TPU v7x, 32 devices: a whole 2x2x4 slice. The times are simulated.
32 devices in a mesh: seq: 4 (over z), head: 2 (over core), dp: 4 (over y, x).
Axes of the slice: x: 2, y: 2, z: 4, core: 2. Of those that a mesh axis runs over, the one named last changes fastest.
Arguments:
- hidden: bfloat16 [4, 768, 1024], P('dp', 'seq'), may hold values from -6 to 6
- norm_gain: float32 [1024], replicated, may hold values from 0.5 to 1.5
- projection: bfloat16 [3, 1024, 1024], P(None, None, 'head'), may hold values from -1 to 1
- upstream: bfloat16 [4, 768, 1024], P('dp', 'seq', 'head'), may hold values from -6 to 6
- cluster: int32 [4, 768, 1], P('dp', 'seq'), may hold values from 0 to 3; in each aligned block of 192 rows (0 to 191, 192 to 383, ..., all dimensions but the last counted through in order) at most 144 rows name the same one
Outputs:
- input_gradient: bfloat16 [4, 768, 1024], P('dp', 'seq', 'head')
- gain_gradient: float32 [1024], P('head')
Inputs may be any that keep to these rules, and one draw needn't show every extreme that they name: Among the 192 tokens of one device no cluster is named more than 144 times, a bound that some block reaches.
All inputs are finite; a program needn't handle non-finite values.
Results may differ from a plain program's by a relative error of at most 0.01.
The roundings to bfloat16 on the way count: a program that leaves them out, or rounds other values in their place, can miss the bound.
Values may be sent and summed in bfloat16 or wider, within the bound.
A program may use at most 64 MiB of HBM per device.

v0:
```python
import jax
import jax.numpy as jnp
from jax import lax
from jax.sharding import PartitionSpec as P

HDIM = 64
CLUS_DEV = 1


epsilon = 1e-05
masked = -1e30


def normalize(values, norm_gain):
    values = values.astype(jnp.float32)
    center = values - jnp.mean(values, -1, keepdims=True)
    spread = lax.rsqrt(jnp.mean(center * center, -1, keepdims=True) + epsilon)
    scaled = center * spread
    return (scaled, spread, (scaled * norm_gain).astype(jnp.bfloat16))


def attend_backward(queries, key_rows, values, upstream, allowed, factor):
    scores = (
        lax.dot_general(
            queries, key_rows, (((1,), (1,)), ((), ())), preferred_element_type=jnp.float32
        )
        * factor
    )
    scores = jnp.where(allowed, scores, masked)
    powers = jnp.exp(scores - jnp.max(scores, -1, keepdims=True))
    weights = powers / jnp.sum(powers, -1, keepdims=True)
    rounded = weights.astype(jnp.bfloat16)
    output = jnp.dot(rounded, values, preferred_element_type=jnp.float32)
    center_term = jnp.sum(upstream.astype(jnp.float32) * output, -1, keepdims=True)
    grad_values = lax.dot_general(
        rounded, upstream, (((0,), (0,)), ((), ())), preferred_element_type=jnp.float32
    ).astype(jnp.bfloat16)
    grad_weights = lax.dot_general(
        upstream, values, (((1,), (1,)), ((), ())), preferred_element_type=jnp.float32
    )
    grad_scores = (weights * (grad_weights - center_term) * factor).astype(jnp.bfloat16)
    grad_queries = jnp.dot(grad_scores, key_rows, preferred_element_type=jnp.float32).astype(
        jnp.bfloat16
    )
    grad_keys = lax.dot_general(
        grad_scores, queries, (((0,), (0,)), ((), ())), preferred_element_type=jnp.float32
    ).astype(jnp.bfloat16)
    return (grad_queries, grad_keys, grad_values)


def cluster_grads(payload, validity, head_width):
    row_count = payload.shape[0]
    spans = payload.shape[1] // 4
    heads_local = spans // head_width
    positions = lax.broadcasted_iota(jnp.int32, (row_count, row_count), 0)
    others = lax.broadcasted_iota(jnp.int32, (row_count, row_count), 1)
    allowed = (positions >= others) & (validity[None, :] > 0)
    factor = head_width ** (-0.5)

    def one_head(head_index, result):
        offset = head_index * head_width

        def select(portion):
            return lax.dynamic_slice_in_dim(payload, portion * spans + offset, head_width, 1)

        grads_head = attend_backward(select(0), select(1), select(2), select(3), allowed, factor)
        for portion in range(3):
            result = lax.dynamic_update_slice_in_dim(
                result, grads_head[portion], portion * spans + offset, 1
            )
        return result

    return lax.fori_loop(0, heads_local, one_head, jnp.zeros((row_count, 3 * spans), jnp.bfloat16))


def on_device(hidden, norm_gain, projection, upstream, cluster):
    seq_count = lax.axis_size("seq")
    tokens = hidden.shape[1]
    width_model = hidden.shape[2]
    spans = projection.shape[2]
    clusters_all = CLUS_DEV * seq_count
    slot_rows = 3 * tokens // clusters_all
    scaled, spread, normed = normalize(hidden[0], norm_gain)
    labels = cluster[0, :, 0]
    member = (labels[:, None] == jnp.arange(clusters_all, dtype=jnp.int32)[None, :]).astype(
        jnp.int32
    )
    ranks = jnp.sum(jnp.cumsum(member, 0) * member, 1) - 1
    target = labels * slot_rows + ranks
    projected = jnp.einsum(
        "td,kdh->tkh", normed, projection, preferred_element_type=jnp.float32
    ).astype(jnp.bfloat16)
    payload = jnp.concatenate([projected.reshape(tokens, 3 * spans), upstream[0]], 1)
    columns = payload.shape[1]
    outgoing = jnp.zeros((clusters_all * slot_rows, columns), jnp.bfloat16).at[target].set(payload)
    outgoing = outgoing.reshape(seq_count, CLUS_DEV, slot_rows, columns)
    present = jnp.zeros((clusters_all * slot_rows,), jnp.bfloat16).at[target].set(1.0)
    present = present.reshape(seq_count, CLUS_DEV, slot_rows)
    rows_in = lax.all_to_all(outgoing, "seq", split_axis=0, concat_axis=0, tiled=True)
    marks_in = lax.all_to_all(present, "seq", split_axis=0, concat_axis=0, tiled=True)
    sources = rows_in.shape[0]
    item_count = rows_in.shape[1]
    stacked = jnp.swapaxes(rows_in, 0, 1).reshape(item_count, sources * slot_rows, rows_in.shape[3])
    mark_rows = jnp.swapaxes(marks_in, 0, 1).reshape(item_count, sources * slot_rows)

    def per_item(entries):
        return cluster_grads(entries[0], entries[1].astype(jnp.float32), HDIM)

    results = lax.map(per_item, (stacked, mark_rows))
    results = jnp.einsum(
        "irkh,kdh->ird",
        results.reshape(item_count, sources * slot_rows, 3, spans),
        projection,
        preferred_element_type=jnp.float32,
    ).astype(jnp.bfloat16)
    width_out = results.shape[-1]
    results = results.reshape(item_count, sources, slot_rows, width_out)
    answer = jnp.swapaxes(results, 0, 1)
    returned = lax.all_to_all(answer, "seq", split_axis=0, concat_axis=0, tiled=True)
    restored = returned.reshape(clusters_all * slot_rows, width_model)[target]
    partial_value = restored.astype(jnp.float32)
    half_width = width_model // lax.axis_size("head")
    offset = lax.axis_index("head") * half_width
    own_scaled = lax.dynamic_slice_in_dim(scaled, offset, half_width, 1)
    own_gain = lax.dynamic_slice_in_dim(norm_gain, offset, half_width, 0)
    gradient = lax.psum_scatter(
        partial_value.astype(jnp.bfloat16), "head", scatter_dimension=1, tiled=True
    ).astype(jnp.float32)
    scaled_grad = gradient * own_gain
    first_sum, second_sum = lax.psum(
        (
            jnp.sum(scaled_grad, -1, keepdims=True),
            jnp.sum(scaled_grad * own_scaled, -1, keepdims=True),
        ),
        "head",
    )
    first_mean = first_sum / width_model
    second_mean = second_sum / width_model
    input_gradient = (spread * (scaled_grad - first_mean - own_scaled * second_mean)).astype(
        jnp.bfloat16
    )
    local_sum = jnp.sum(gradient * own_scaled, 0)
    gain_total = lax.psum(local_sum, ("seq", "dp"))
    gain_gradient = gain_total * (seq_count * lax.axis_size("dp") * tokens) ** (-0.5)
    return (input_gradient.reshape(1, tokens, half_width), gain_gradient)


def solution(mesh):
    in_specs = (
        P("dp", "seq", None),
        P(),
        P(None, None, "head"),
        P("dp", "seq", "head"),
        P("dp", "seq", None),
    )
    out_specs = (P("dp", "seq", "head"), P("head"))
    return jax.shard_map(
        on_device, mesh=mesh, in_specs=in_specs, out_specs=out_specs, check_vma=False
    )
```

profile of v0, /device:TPU:0, one launch (start us, length us, event | category | flops | bytes accessed | tf_op | source)
XLA Modules:
  0.0 309.7 jit_solution(8986119475946136474)
XLA Ops:
  13.5 6.3 %all-to-all-start.1 = ((bf16[4,1,144]{2,1,0:T(2,128)(2,1)}), bf16[4,1,144]{2,1,0:T(2,128)(2,1)S(1)}, u32[]{:S(2)}, u32[]{:S(2)}) async-start(bf16[4,1,144]{2,1,0:T(2,128)(2,1)} %reshape.138), calls=%async_computation.1 | async-start | bytes 8192 | tf_op jit(solution)/shard_map/all_to_all | solution.py:100
  25.1 4.1 %scatter_custom_fusion = bf16[576,2048]{1,0:T(8,128)(2,1)} fusion(s32[192]{0:T(256)S(1)} %bitcast.81, bf16[]{:T(256)} %constant.178.clone.1, bf16[192,512]{1,0:T(8,128)(2,1)S(1)} %bitcast.72, bf16[]{:T(256)} %constant.195, bf16[192,1536]{1,0:T(8,128)(2,1)} %bitcast.69), kind=kCustom, calls=%fused_computation.37 | custom fusion | flops 1572864 | bytes 3145732 | tf_op jit(solution)/shard_map/scatter | solution.py:95
  29.1 5.1 %all-to-all-start = ((bf16[4,1,144,2048]{3,2,1,0:T(8,128)(2,1)}), bf16[4,1,144,2048]{3,2,1,0:T(8,128)(2,1)}, u32[]{:S(2)}, u32[]{:S(2)}) async-start(bf16[4,1,144,2048]{3,2,1,0:T(8,128)(2,1)} %bitcast.68), calls=%async_computation | async-start | bytes 4718592 | tf_op jit(solution)/shard_map/all_to_all | solution.py:99
  34.3 53.2 %all-to-all-done = bf16[4,1,144,2048]{3,2,1,0:T(8,128)(2,1)} async-done(((bf16[4,1,144,2048]{3,2,1,0:T(8,128)(2,1)}), bf16[4,1,144,2048]{3,2,1,0:T(8,128)(2,1)}, u32[]{:S(2)}, u32[]{:S(2)}) %all-to-all-start) | async-done | bytes 2359328 | tf_op jit(solution)/shard_map/all_to_all | solution.py:99
  87.6 4.3 %copy.24 = bf16[576,2048]{0,1:T(8,128)(2,1)} copy(bf16[576,2048]{1,0:T(8,128)(2,1)} %bitcast.11) | data formatting | bytes 4718592
  93.3 113.3 %while.24 = (s32[]{:T(128)}, bf16[576,1536]{0,1:T(8,128)(2,1)}, bf16[576,2048]{0,1:T(8,128)(2,1)}, pred[576]{0:T(1024)(128)(4,1)S(1)}, s32[]{:T(128)}, /*index=5...) while((s32[]{:T(128)}, bf16[576,1536]{0,1:T(8,128)(2,1)}, ...), condition=%wide.region_11.12_spmd.clone, body=%wide.region_7.11_spmd.clone.sunk | while | flops 260331856 | bytes 16045296 | solution.py:73
  98.3 2.9 multiply_convert_fusion.3
  103.3 2.1 fusion.90
  105.4 2.1 fusion.91
  112.5 2.9 multiply_convert_fusion.3
  119.5 2.1 fusion.91
  126.7 2.9 multiply_convert_fusion.3
  131.6 2.1 fusion.90
  133.7 2.1 fusion.91
  140.9 2.9 multiply_convert_fusion.3
  147.9 2.1 fusion.91
  155.0 2.9 multiply_convert_fusion.3
  159.9 2.1 fusion.90
  169.2 2.9 multiply_convert_fusion.3
  174.1 2.1 fusion.90
  183.3 2.9 multiply_convert_fusion.3
  188.3 2.1 fusion.90
  197.5 2.9 multiply_convert_fusion.3
  202.4 2.1 fusion.90
  204.5 2.1 fusion.91
  206.6 5.0 %bitcast_convert_fusion = bf16[576,1024]{1,0:T(8,128)(2,1)} fusion(bf16[576,3,512]{0,2,1:T(8,128)(2,1)} %bitcast.70, bf16[3,1024,512]{2,1,0:T(8,128)(2,1)S(1)} %copy-done), kind=kOutput, calls=%fused_computation.34 | convolution fusion | flops 1812529152 | bytes 6094848 | tf_op jit(solution)/shard_map/irkh,kdh->ird/dot_general | solution.py:110
  211.6 4.3 %all-to-all-start.2 = ((bf16[4,1,144,1024]{3,2,1,0:T(8,128)(2,1)}), bf16[4,1,144,1024]{3,2,1,0:T(8,128)(2,1)}, u32[]{:S(2)}, u32[]{:S(2)}) async-start(bf16[4,1,144,1024]{3,2,1,0:T(8,128)(2,1)} %bitcast.71), calls=%async_computation.2 | async-start | bytes 2359296 | tf_op jit(solution)/shard_map/all_to_all | solution.py:119
  215.9 28.1 %all-to-all-done.2 = bf16[4,1,144,1024]{3,2,1,0:T(8,128)(2,1)} async-done(((bf16[4,1,144,1024]{3,2,1,0:T(8,128)(2,1)}), bf16[4,1,144,1024]{3,2,1,0:T(8,128)(2,1)}, u32[]{:S(2)}, u32[]{:S(2)}) %all-to-all-start.2) | async-done | bytes 1179680 | tf_op jit(solution)/shard_map/all_to_all | solution.py:119
  244.0 3.5 %gather_fusion = bf16[192,1024]{1,0:T(8,128)(2,1)} fusion(bf16[576,1024]{1,0:T(8,128)(2,1)} %bitcast.16, s32[1024]{0:T(1024)S(1)} %pad_clamp_fusion), kind=kCustom, calls=%fused_computation | custom fusion | bytes 787200 | tf_op jit(solution)/shard_map/gather | solution.py:120
  248.8 5.8 %reduce-scatter.2.cloned.1.call-done = bf16[192,512]{1,0:T(8,128)(2,1)} async-done(((bf16[192,1024]{1,0:T(8,128)(2,1)}), bf16[192,512]{1,0:T(8,128)(2,1)}) %reduce-scatter.2.cloned.1.call-update) | async-done | bytes 196624 | tf_op jit(solution)/shard_map/reduce_scatter | solution.py:126
  256.0 41.9 %psum.23 = f32[512]{0:T(512)S(1)} all-reduce(f32[512]{0:T(512)S(1)} %get-tuple-element.173), channel_id=1, replica_groups=mesh['seq'=4,'head'=2,'dp'=4] {'seq','dp'}, use_global_device_ids=true, to_apply=%region_18.19 | all-reduce | flops 512 | bytes 4096 | tf_op jit(solution)/shard_map/psum | solution.py:143
  298.5 2.4 all-reduce.1
  (105 shorter events, 85.2 us)
Async XLA Ops:
  7.2 15.1 %copy-start = (bf16[3,1024,512]{2,1,0:T(8,128)(2,1)S(1)}, bf16[3,1024,512]{2,1,0:T(8,128)(2,1)}, u32[]{:S(2)}) copy-start(bf16[3,1024,512]{2,1,0:T(8,128)(2,1)} %param.9) | copy-start | bytes 9437188
  13.5 15.6 %all-to-all-start.1 = ((bf16[4,1,144]{2,1,0:T(2,128)(2,1)}), bf16[4,1,144]{2,1,0:T(2,128)(2,1)S(1)}, u32[]{:S(2)}, u32[]{:S(2)}) async-start(bf16[4,1,144]{2,1,0:T(2,128)(2,1)} %reshape.138), calls=%async_computation.1 | async-start | bytes 8192 | tf_op jit(solution)/shard_map/all_to_all | solution.py:100
  22.3 2.8 copy-start.3
  29.1 58.5 %all-to-all-start = ((bf16[4,1,144,2048]{3,2,1,0:T(8,128)(2,1)}), bf16[4,1,144,2048]{3,2,1,0:T(8,128)(2,1)}, u32[]{:S(2)}, u32[]{:S(2)}) async-start(bf16[4,1,144,2048]{3,2,1,0:T(8,128)(2,1)} %bitcast.68), calls=%async_computation | async-start | bytes 4718592 | tf_op jit(solution)/shard_map/all_to_all | solution.py:99
  94.7 1.2 copy-start.1
  108.8 1.2 copy-start.1
  123.0 1.2 copy-start.1
  137.2 1.2 copy-start.1
  151.3 1.2 copy-start.1
  165.5 1.2 copy-start.1
  179.6 1.2 copy-start.1
  193.8 1.2 copy-start.1
  211.6 32.4 %all-to-all-start.2 = ((bf16[4,1,144,1024]{3,2,1,0:T(8,128)(2,1)}), bf16[4,1,144,1024]{3,2,1,0:T(8,128)(2,1)}, u32[]{:S(2)}, u32[]{:S(2)}) async-start(bf16[4,1,144,1024]{3,2,1,0:T(8,128)(2,1)} %bitcast.71), calls=%async_computation.2 | async-start | bytes 2359296 | tf_op jit(solution)/shard_map/all_to_all | solution.py:119
  215.9 38.8 %reduce-scatter.2.cloned.1.call-start = ((), (), s32[]{:S(2)}) async-start(), calls=%async_computation.4 | async-start | bytes 589824 | tf_op jit(solution)/shard_map/reduce_scatter | solution.py:126
  244.0 3.6 %copy-start.4 = (f32[1024]{0:T(1024)S(1)}, f32[1024]{0:T(1024)}, u32[]{:S(2)}) copy-start(f32[1024]{0:T(1024)} %param.8) | copy-start | bytes 12292
  244.0 3.7 %copy-start.2 = (bf16[1,192,1024]{2,1,0:T(8,128)(2,1)S(1)}, bf16[1,192,1024]{2,1,0:T(8,128)(2,1)}, u32[]{:S(2)}) copy-start(bf16[1,192,1024]{2,1,0:T(8,128)(2,1)} %param.7) | copy-start | bytes 1179652
Sparse Core Ops, SparseCore 0:
  247.7 6.8 reduce-scatter.1
where the time goes:
time: 312 us; the launch traced here: 310 us
  matrix products  102 us (33%)
  waiting for transfers between devices  87.2 us (28%)
  blocking collectives  44.4 us (14%)
  other arithmetic  25.9 us (8%)
  local copies, waits for them, and re-layouts  20.4 us (7%)
  starting transfers between devices  15.7 us (5%)
  between operations  14.1 us (5%)
    all_to_all x1, waiting for transfers between devices, on_device(): lax.all_to_all(outgoing, 'seq', split_axis=0, concat_axis=0, tiled=True)  53.2 us
    psum x1, blocking collectives, on_device(): gain_total = lax.psum(local_sum, ('seq', 'dp'))  41.9 us
    all_to_all x1, waiting for transfers between devices, on_device(): lax.all_to_all(answer, 'seq', split_axis=0, concat_axis=0, tiled=True)  28.1 us
    dot_general x8, matrix products, attend_backward(): lax.dot_general(upstream, values, (((1,), (1,)), ((), ())), preferred_ele...  22.9 us
    dot_general x8, matrix products, attend_backward(): lax.dot_general(grad_scores, queries, (((0,), (0,)), ((), ())), preferred...  16.8 us
    dot_general x8, matrix products, attend_backward(): lax.dot_general(rounded, upstream, (((0,), (0,)), ((), ())), preferred_el...  16.8 us
    dot_general x8, matrix products, attend_backward(): jnp.dot(grad_scores, key_rows, preferred_element_type=jnp.float32)  16.4 us
    dot_general x8, matrix products, attend_backward(): output = jnp.dot(rounded, values, preferred_element_type=jnp.float32)  11.3 us
  transfers between devices with their start and end apart: 4, of which 3 were waited for; matrix products, arithmetic and copies ran while one was open for 3% of the time, Pallas kernels for 0%

commit v1 on v0

--- a/solution.py
+++ b/solution.py
@@ -1,6 +1,10 @@
+import functools
+
 import jax
 import jax.numpy as jnp
 from jax import lax
+from jax.experimental import pallas as pl
+from jax.experimental.pallas import tpu as pltpu
 from jax.sharding import PartitionSpec as P
 
 HDIM = 64
@@ -145,6 +149,325 @@
     return (input_gradient.reshape(1, tokens, half_width), gain_gradient)
 
 
+MESH = pl.DeviceIdType.MESH
+LANES = 128
+ROW_BLOCK = 256
+NT = (((1,), (1,)), ((), ()))
+TN = (((0,), (0,)), ((), ()))
+
+
+def dot(left, right, dims=(((1,), (0,)), ((), ()))):
+    return lax.dot_general(left, right, dims, preferred_element_type=jnp.float32)
+
+
+def fused(
+    n_seq, n_head, n_dp, total_rows,
+    hidden_ref, gain_ref, proj_hbm, up_ref, label_ref,
+    grad_ref, gain_out_ref,
+    w_ref, scaled_ref, snd, rcv, labels_in, onehot, weights, acc_v, acc_k, gsend, gback,
+    part_out, part_in, gain_src, gain_dp, gain_mid, gain_seq,
+    w_sem, f_send, f_recv, l_send, l_recv, b_send, b_recv, h_send, h_recv,
+    d_send, d_recv, s_send, s_recv,
+):
+    me = lax.axis_index("seq")
+    core = lax.axis_index("head")
+    group = lax.axis_index("dp")
+    tokens, width = hidden_ref.shape
+    spans = up_ref.shape[1]
+    length = n_seq * tokens
+    half = width // n_head
+    heads = LANES // HDIM
+    factor = HDIM ** (-0.5)
+
+    w_copies = [pltpu.make_async_copy(proj_hbm.at[p], w_ref.at[p], w_sem.at[p]) for p in range(3)]
+    for copy in w_copies:
+        copy.start()
+    barrier = pltpu.get_barrier_semaphore()
+    peers = [("seq", me, n_seq), ("head", core, n_head), ("dp", group, n_dp)]
+    for axis, index, size in peers:
+        for o in range(1, size):
+            pl.semaphore_signal(
+                barrier, inc=1, device_id={axis: lax.rem(index + o, size)}, device_id_type=MESH
+            )
+
+    def remote(src, dst, send, recv, axis, index):
+        return pltpu.make_async_remote_copy(
+            src_ref=src, dst_ref=dst, send_sem=send, recv_sem=recv,
+            device_id={axis: index}, device_id_type=MESH,
+        )
+
+    def rows_of(index):
+        return pl.ds(pl.multiple_of(index * tokens, 16), tokens)
+
+    def lanes_of(index):
+        return pl.ds(pl.multiple_of(index * LANES, LANES), LANES)
+
+    my_rows = rows_of(me)
+    forward, label_copies = {}, []
+    for o in range(1, n_seq):
+        j = lax.rem(me + o, n_seq)
+        for kind in range(4):
+            src = up_ref.at[:, lanes_of(j)] if kind == 0 else snd.at[kind - 1, j]
+            forward[kind, o] = remote(
+                src, rcv.at[kind, my_rows], f_send.at[kind, o - 1], f_recv.at[kind, o - 1], "seq", j
+            )
+        label_copies.append(
+            remote(label_ref, labels_in.at[me], l_send.at[o - 1], l_recv.at[o - 1], "seq", j)
+        )
+
+    values = hidden_ref[...].astype(jnp.float32)
+    center = values - jnp.mean(values, -1, keepdims=True)
+    spread = lax.rsqrt(jnp.mean(center * center, -1, keepdims=True) + epsilon)
+    scaled = center * spread
+    scaled_ref[...] = scaled
+    normed = (scaled * gain_ref[...]).astype(jnp.bfloat16)
+
+    pl.semaphore_wait(barrier, n_seq + n_head + n_dp - 3)
+    for copy in label_copies:
+        copy.start()
+    for o in range(1, n_seq):
+        forward[0, o].start()
+    rcv[0, my_rows, :] = up_ref[:, lanes_of(me)]
+    labels_in[me] = label_ref[...]
+    for p in range(3):
+        w_copies[p].wait()
+        made = dot(normed, w_ref[p]).astype(jnp.bfloat16)
+        for j in range(n_seq):
+            snd[p, j] = made[:, j * LANES : (j + 1) * LANES]
+        for o in range(1, n_seq):
+            forward[p + 1, o].start()
+        rcv[p + 1, my_rows, :] = snd[p, me]
+
+    for copy in label_copies:
+        copy.wait_recv()
+    labels = labels_in[0]
+    for j in range(1, n_seq):
+        labels = labels + labels_in[j]
+    classes = lax.broadcasted_iota(jnp.int32, (onehot.shape[0], LANES), 0).astype(jnp.float32)
+    for c in range(length // LANES):
+        hit = classes == labels[c : c + 1, :]
+        onehot[:, c * LANES : (c + 1) * LANES] = jnp.where(hit, 1.0, 0.0).astype(jnp.bfloat16)
+
+    lane_head = lax.broadcasted_iota(jnp.int32, (1, LANES), 1) // HDIM
+    head_masks = [jnp.where(lane_head == h, 1.0, 0.0).astype(jnp.bfloat16) for h in range(heads)]
+    blocks = list(reversed(range(length // ROW_BLOCK)))
+
+    def arrived(kind):
+        for o in range(1, n_seq):
+            forward[kind, o].wait_recv()
+
+    def send_back(portion):
+        copies = []
+        for o in range(1, n_seq):
+            j = lax.rem(me + o, n_seq)
+            copy = remote(
+                gsend.at[portion, rows_of(j)], gback.at[portion, :, lanes_of(me)],
+                b_send.at[portion, o - 1], b_recv.at[portion, o - 1], "seq", j,
+            )
+            copy.start()
+            copies.append(copy)
+        gback[portion, :, lanes_of(me)] = gsend[portion, my_rows, :]
+        return copies
+
+    for kind in (0, 1, 2):
+        arrived(kind)
+    for block in blocks:
+        first, reach = block * ROW_BLOCK, (block + 1) * ROW_BLOCK
+        same = dot(onehot[:, first:reach], onehot[:, :reach], TN)
+        row_at = lax.broadcasted_iota(jnp.int32, (ROW_BLOCK, reach), 0) + first
+        col_at = lax.broadcasted_iota(jnp.int32, (ROW_BLOCK, reach), 1)
+        allowed = (same > 0.5) & (row_at >= col_at)
+        for h in range(heads):
+            query = rcv[1, first:reach, :] * head_masks[h]
+            scores = dot(query, rcv[2, :reach, :], NT) * factor
+            scores = jnp.where(allowed, scores, masked)
+            powers = jnp.exp(scores - jnp.max(scores, -1, keepdims=True))
+            weight = powers * (1.0 / jnp.sum(powers, -1, keepdims=True))
+            weights[h, first:reach, :reach] = weight
+            term = dot(weight.astype(jnp.bfloat16), rcv[0, first:reach, :] * head_masks[h], TN)
+            if block == blocks[0] and h == 0:
+                acc_v[...] = term
+            else:
+                acc_v[:reach, :] += term
+    gsend[2] = acc_v[...].astype(jnp.bfloat16)
+    back = {2: send_back(2)}
+
+    arrived(3)
+    for block in blocks:
+        first, reach = block * ROW_BLOCK, (block + 1) * ROW_BLOCK
+        grad_query = None
+        for h in range(heads):
+            weight = weights[h, first:reach, :reach]
+            cotangent = rcv[0, first:reach, :] * head_masks[h]
+            output = dot(weight.astype(jnp.bfloat16), rcv[3, :reach, :])
+            middle = jnp.sum(cotangent.astype(jnp.float32) * output, -1, keepdims=True)
+            grad_weights = dot(cotangent, rcv[3, :reach, :], NT)
+            grad_scores = (weight * (grad_weights - middle) * factor).astype(jnp.bfloat16)
+            found = dot(grad_scores, rcv[2, :reach, :])
+            grad_query = found if h == 0 else jnp.where(lane_head == h, found, grad_query)
+            term = dot(grad_scores, rcv[1, first:reach, :] * head_masks[h], TN)
+            if block == blocks[0] and h == 0:
+                acc_k[...] = term
+            else:
+                acc_k[:reach, :] += term
+        gsend[0, first:reach, :] = grad_query.astype(jnp.bfloat16)
+    back[0] = send_back(0)
+    gsend[1] = acc_k[...].astype(jnp.bfloat16)
+    back[1] = send_back(1)
+
+    for portion in (2, 0, 1):
+        for copy in back[portion]:
+            copy.wait_recv()
+    exchanges = []
+    for c in range(2):
+        cut = slice(c * width // 2, (c + 1) * width // 2)
+        partial = dot(gback[0], w_ref[0, cut, :], NT)
+        for p in (1, 2):
+            partial = partial + dot(gback[p], w_ref[p, cut, :], NT)
+        part_out[c] = partial.astype(jnp.bfloat16)
+        copy = remote(
+            part_out.at[c], part_in.at[c], h_send.at[c], h_recv.at[c], "head", lax.rem(core + 1, n_head)
+        )
+        copy.start()
+        exchanges.append(copy)
+
+    gradients, first_sum, second_sum = [], 0.0, 0.0
+    for c in range(2):
+        cut = slice(c * width // 2, (c + 1) * width // 2)
+        exchanges[c].wait_recv()
+        gradient = part_out[c].astype(jnp.float32) + part_in[c].astype(jnp.float32)
+        scaled_grad = gradient * gain_ref[:, cut]
+        own_scaled = scaled_ref[:, cut]
+        first_sum = first_sum + jnp.sum(scaled_grad, -1, keepdims=True)
+        second_sum = second_sum + jnp.sum(scaled_grad * own_scaled, -1, keepdims=True)
+    own_cut = pl.ds(pl.multiple_of(core * half, LANES), half)
+    gradient = part_out[core].astype(jnp.float32) + part_in[core].astype(jnp.float32)
+    own_scaled = scaled_ref[:, own_cut]
+    local_sum = jnp.sum(gradient * own_scaled, 0, keepdims=True)
+    gain_src[...] = jnp.zeros_like(gain_src)
+    for c in range(half // LANES):
+        gain_src[c : c + 1, :] = local_sum[:, c * LANES : (c + 1) * LANES]
+    over_dp = []
+    for o in range(1, n_dp):
+        copy = remote(
+            gain_src, gain_dp.at[group], d_send.at[o - 1], d_recv.at[o - 1],
+            "dp", lax.rem(group + o, n_dp),
+        )
+        copy.start()
+        over_dp.append(copy)
+    gain_dp[group] = gain_src[...]
+    scaled_grad = gradient * gain_ref[:, own_cut]
+    first_mean = first_sum / width
+    second_mean = second_sum / width
+    again = hidden_ref[...].astype(jnp.float32)
+    again = again - jnp.mean(again, -1, keepdims=True)
+    spread = lax.rsqrt(jnp.mean(again * again, -1, keepdims=True) + epsilon)
+    grad_ref[...] = (spread * (scaled_grad - first_mean - own_scaled * second_mean)).astype(
+        jnp.bfloat16
+    )
+    for copy in over_dp:
+        copy.wait_recv()
+    total = gain_dp[0]
+    for j in range(1, n_dp):
+        total = total + gain_dp[j]
+    gain_mid[...] = total
+    over_seq = []
+    for o in range(1, n_seq):
+        copy = remote(
+            gain_mid, gain_seq.at[me], s_send.at[o - 1], s_recv.at[o - 1],
+            "seq", lax.rem(me + o, n_seq),
+        )
+        copy.start()
+        over_seq.append(copy)
+    gain_seq[me] = total
+    for copies in (label_copies, forward.values(), *back.values(), exchanges, over_dp):
+        for copy in copies:
+            copy.wait_send()
+    for copy in over_seq:
+        copy.wait()
+    total = gain_seq[0]
+    for j in range(1, n_seq):
+        total = total + gain_seq[j]
+    gain_out_ref[...] = total * total_rows ** (-0.5)
+
+
+def on_device_heads(hidden, norm_gain, projection, upstream, cluster):
+    n_seq, n_head, n_dp = (lax.axis_size(a) for a in ("seq", "head", "dp"))
+    tokens, width = hidden.shape[1:]
+    spans = projection.shape[2]
+    length = n_seq * tokens
+    heads = LANES // HDIM
+    half = width // n_head
+    label_rows = -(-length // (8 * LANES)) * 8
+    class_rows = -(-(CLUS_DEV * n_seq) // 16) * 16
+    labels = lax.dynamic_update_slice(
+        jnp.zeros((label_rows * LANES,), jnp.float32),
+        cluster[0, :, 0].astype(jnp.float32),
+        (lax.axis_index("seq") * tokens,),
+    ).reshape(label_rows, LANES)
+    gain_rows = -(-half // (8 * LANES)) * 8
+    vmem = pl.BlockSpec(memory_space=pltpu.VMEM)
+    dma = pltpu.SemaphoreType.DMA
+    bf16, f32 = jnp.bfloat16, jnp.float32
+    gradient, gain = pl.pallas_call(
+        functools.partial(fused, n_seq, n_head, n_dp, n_seq * n_dp * tokens),
+        out_shape=(
+            jax.ShapeDtypeStruct((tokens, half), bf16),
+            jax.ShapeDtypeStruct((gain_rows, LANES), f32),
+        ),
+        in_specs=[vmem, vmem, pl.BlockSpec(memory_space=pl.ANY), vmem, vmem],
+        out_specs=(vmem, vmem),
+        scratch_shapes=[
+            pltpu.VMEM((3, width, spans), bf16),
+            pltpu.VMEM((tokens, width), f32),
+            pltpu.VMEM((3, n_seq, tokens, LANES), bf16),
+            pltpu.VMEM((4, length, LANES), bf16),
+            pltpu.VMEM((n_seq, label_rows, LANES), f32),
+            pltpu.VMEM((class_rows, length), bf16),
+            pltpu.VMEM((heads, length, length), f32),
+            pltpu.VMEM((length, LANES), f32),
+            pltpu.VMEM((length, LANES), f32),
+            pltpu.VMEM((3, length, LANES), bf16),
+            pltpu.VMEM((3, tokens, spans), bf16),
+            pltpu.VMEM((2, tokens, width // 2), bf16),
+            pltpu.VMEM((2, tokens, width // 2), bf16),
+            pltpu.VMEM((gain_rows, LANES), f32),
+            pltpu.VMEM((n_dp, gain_rows, LANES), f32),
+            pltpu.VMEM((gain_rows, LANES), f32),
+            pltpu.VMEM((n_seq, gain_rows, LANES), f32),
+            dma((3,)),
+            dma((4, n_seq - 1)),
+            dma((4, n_seq - 1)),
+            dma((n_seq - 1,)),
+            dma((n_seq - 1,)),
+            dma((3, n_seq - 1)),
+            dma((3, n_seq - 1)),
+            dma((2,)),
+            dma((2,)),
+            dma((n_dp - 1,)),
+            dma((n_dp - 1,)),
+            dma((n_seq - 1,)),
+            dma((n_seq - 1,)),
+        ],
+        compiler_params=pltpu.CompilerParams(collective_id=0, has_side_effects=True),
+    )(hidden[0], norm_gain[None, :], projection, upstream[0], labels)
+    gain_gradient = gain[: half // LANES].reshape(half)
+    return (gradient.reshape(1, tokens, half), gain_gradient)
+
+
+def splits_by_heads(mesh, hidden, projection):
+    n_seq, n_head, n_dp = (mesh.shape[a] for a in ("seq", "head", "dp"))
+    spans = projection.shape[2] // n_head
+    return (
+        n_head == 2
+        and n_dp > 1
+        and n_seq > 1
+        and spans == n_seq * LANES
+        and hidden.shape[1] % ROW_BLOCK == 0
+        and hidden.shape[1] <= 4 * ROW_BLOCK
+    )
+
+
 def solution(mesh):
     in_specs = (
         P("dp", "seq", None),
@@ -154,6 +477,11 @@
         P("dp", "seq", None),
     )
     out_specs = (P("dp", "seq", "head"), P("head"))
-    return jax.shard_map(
-        on_device, mesh=mesh, in_specs=in_specs, out_specs=out_specs, check_vma=False
-    )
+
+    def program(hidden, norm_gain, projection, upstream, cluster):
+        body = on_device_heads if splits_by_heads(mesh, hidden, projection) else on_device
+        return jax.shard_map(
+            body, mesh=mesh, in_specs=in_specs, out_specs=out_specs, check_vma=False
+        )(hidden, norm_gain, projection, upstream, cluster)
+
+    return program

time: 312 us -> 55.4 us (0.18)
  matrix products: 102 us -> 0 us
  waiting for transfers between devices: 87.2 us -> 0 us
  Pallas kernels: 0 us -> 50.2 us
  blocking collectives: 44.4 us -> 0 us
  other arithmetic: 25.9 us -> 0.68 us
  local copies, waits for them, and re-layouts: 20.4 us -> 3.64 us
  starting transfers between devices: 15.7 us -> 0 us
  between operations: 14.1 us -> 0.65 us
    dot_general x50 -> x0, matrix products: 102 us -> none  [the longest x8 22.9 us: attend_backward(): lax.dot_general(upstream, values, (((1,), (1,)), ((), ())), preferred_ele...]
    all_to_all x3 -> x0, waiting for transfers between devices: 81.3 us -> none  [the longest x1 53.2 us: on_device(): lax.all_to_all(outgoing, 'seq', split_axis=0, concat_axis=0, tiled=True)]
    pallas_call x0 -> x1, Pallas kernels: none -> 50.2 us  [on_device_heads(): pl.pallas_call(functools.partial(fused, n_seq, n_head, n_dp, n_seq * n_dp...]
    psum x2 -> x0, blocking collectives: 44.4 us -> none  [the longest x1 41.9 us: on_device(): gain_total = lax.psum(local_sum, ('seq', 'dp'))]
    all_to_all x3 -> x0, starting transfers between devices: 15.7 us -> none  [the longest x1 6.35 us: on_device(): lax.all_to_all(present, 'seq', split_axis=0, concat_axis=0, tiled=True)]
    convert_element_type x8 -> x1, other arithmetic: 8.93 us -> 0.68 us  [on_device_heads(): cluster[0, :, 0].astype(jnp.float32)]
    while x16 -> x0, local copies, waits for them, and re-layouts: 7.29 us -> none
    reduce_sum x12 -> x0, other arithmetic: 6.38 us -> none  [the longest x8 1.98 us: attend_backward(): weights = powers / jnp.sum(powers, -1, keepdims=True)]
  transfers between devices with their start and end apart: 4 -> 0, of which waited for: 3 -> 0; matrix products, arithmetic and copies ran while one was open for 3% -> 0% of each run, Pallas kernels for 0% -> 0%
where the time goes in v1:
time: 55.4 us; the launch traced here: 55.2 us
  Pallas kernels  50.2 us (91%)
  local copies, waits for them, and re-layouts  3.64 us (7%)
  other arithmetic  0.68 us (1%)
  between operations  0.65 us (1%)
    pallas_call x1, Pallas kernels, on_device_heads(): pl.pallas_call(functools.partial(fused, n_seq, n_head, n_dp, n_seq * n_dp...  50.2 us
    unnamed x3, local copies, waits for them, and re-layouts  2.21 us
    reshape x1, local copies, waits for them, and re-layouts, on_device_heads(): gain_gradient = gain[:half // LANES].reshape(half)  1.25 us

profile of v1, /device:TPU:0, one launch (start us, length us, event | category | flops | bytes accessed | tf_op | source)
XLA Modules:
  0.0 55.2 jit_solution(12167146915780147583)
XLA Ops:
  0.6 0.7 %convert_element_type.6 = f32[1,192,1]{1,2,0:T(1,128)S(1)} convert(s32[1,192,1]{1,2,0:T(1,128)} %param.9) | non-fusion elementwise | flops 192 | bytes 1536 | tf_op jit(solution)/shard_map/convert_element_type | solution.py:405
  1.3 0.2 dynamic_update_slice.3
  1.5 0.0 copy-start
  1.5 0.6 %copy-done = f32[1024]{0:T(1024)} copy-done((f32[1024]{0:T(1024)}, f32[1024]{0:T(1024)S(1)}, u32[]{:S(2)}) %copy-start) | copy-done | bytes 4120
  2.1 50.2 %shard_map.68 = (bf16[192,512]{1,0:T(8,128)(2,1)}, f32[8,128]{1,0:T(8,128)}) custom-call(bf16[192,1024]{1,0:T(8,128)(2,1)} %bitcast.8, f32[1,1024]{1,0:T(1,128)} %bitcast.12, bf16[3,1024,512]{2,1,0:T(8,128)(2,1)} %proj_hbm.1, bf16[192,512]{1,0:T(8,128)(2,1)} %bitcast.9, f32[8,128]{1,0:T(8,128)} %bitcast.11), custom_call_target="tpu_custom_call" | custom-call | tf_op jit(solution)/shard_map/pallas_call | solution.py:412
  52.3 1.3 %slice_bitcast_fusion = f32[512]{0:T(512)} fusion(f32[8,128]{1,0:T(8,128)} %get-tuple-element.5), kind=kLoop, calls=%fused_computation | loop fusion | bytes 4096 | tf_op jit(solution)/shard_map/reshape | solution.py:454
  53.6 1.6 %copy.9 = bf16[1,192,512]{2,1,0:T(8,128)(2,1)} copy(bf16[1,192,512]{2,1,0:T(8,128)(2,1)} %bitcast.10) | data formatting | bytes 393216
  (1 shorter events, 0.0 us)
Async XLA Ops:
  1.5 0.6 %copy-start = (f32[1024]{0:T(1024)}, f32[1024]{0:T(1024)S(1)}, u32[]{:S(2)}) copy-start(f32[1024]{0:T(1024)S(1)} %dynamic_update_slice.3) | copy-start | bytes 12292

commit v2 on v1

--- a/solution.py
+++ b/solution.py
@@ -165,9 +165,9 @@
     hidden_ref, gain_ref, proj_hbm, up_ref, label_ref,
     grad_ref, gain_out_ref,
     w_ref, scaled_ref, snd, rcv, labels_in, onehot, weights, acc_v, acc_k, gsend, gback,
-    part_out, part_in, gain_src, gain_dp, gain_mid, gain_seq,
+    part_out, part_in, spread_ref, gain_src, gain_seq, gain_mid, gain_all, gain_sum,
     w_sem, f_send, f_recv, l_send, l_recv, b_send, b_recv, h_send, h_recv,
-    d_send, d_recv, s_send, s_recv,
+    s_send, s_recv, d_send, d_recv,
 ):
     me = lax.axis_index("seq")
     core = lax.axis_index("head")
@@ -183,17 +183,18 @@
     for copy in w_copies:
         copy.start()
     barrier = pltpu.get_barrier_semaphore()
-    peers = [("seq", me, n_seq), ("head", core, n_head), ("dp", group, n_dp)]
-    for axis, index, size in peers:
-        for o in range(1, size):
-            pl.semaphore_signal(
-                barrier, inc=1, device_id={axis: lax.rem(index + o, size)}, device_id_type=MESH
-            )
-
-    def remote(src, dst, send, recv, axis, index):
+    along = [{"seq": lax.rem(me + o, n_seq)} for o in range(1, n_seq)]
+    across = [
+        {"dp": lax.rem(group + o // n_head, n_dp), "head": lax.rem(core + o % n_head, n_head)}
+        for o in range(1, n_dp * n_head)
+    ]
+    for peer in along + across:
+        pl.semaphore_signal(barrier, inc=1, device_id=peer, device_id_type=MESH)
+
+    def remote(src, dst, send, recv, peer):
         return pltpu.make_async_remote_copy(
             src_ref=src, dst_ref=dst, send_sem=send, recv_sem=recv,
-            device_id={axis: index}, device_id_type=MESH,
+            device_id=peer, device_id_type=MESH,
         )
 
     def rows_of(index):
@@ -209,24 +210,25 @@
         for kind in range(4):
             src = up_ref.at[:, lanes_of(j)] if kind == 0 else snd.at[kind - 1, j]
             forward[kind, o] = remote(
-                src, rcv.at[kind, my_rows], f_send.at[kind, o - 1], f_recv.at[kind, o - 1], "seq", j
+                src, rcv.at[kind, my_rows], f_send.at[kind, o - 1], f_recv.at[kind, o - 1], along[o - 1]
             )
         label_copies.append(
-            remote(label_ref, labels_in.at[me], l_send.at[o - 1], l_recv.at[o - 1], "seq", j)
+            remote(label_ref, labels_in.at[me], l_send.at[o - 1], l_recv.at[o - 1], along[o - 1])
         )
 
+    pl.semaphore_wait(barrier, len(along) + len(across))
+    for copy in label_copies:
+        copy.start()
+    for o in range(1, n_seq):
+        forward[0, o].start()
     values = hidden_ref[...].astype(jnp.float32)
     center = values - jnp.mean(values, -1, keepdims=True)
     spread = lax.rsqrt(jnp.mean(center * center, -1, keepdims=True) + epsilon)
     scaled = center * spread
     scaled_ref[...] = scaled
+    spread_ref[...] = jnp.broadcast_to(spread, spread_ref.shape)
     normed = (scaled * gain_ref[...]).astype(jnp.bfloat16)
 
-    pl.semaphore_wait(barrier, n_seq + n_head + n_dp - 3)
-    for copy in label_copies:
-        copy.start()
-    for o in range(1, n_seq):
-        forward[0, o].start()
     rcv[0, my_rows, :] = up_ref[:, lanes_of(me)]
     labels_in[me] = label_ref[...]
     for p in range(3):
@@ -256,18 +258,23 @@
         for o in range(1, n_seq):
             forward[kind, o].wait_recv()
 
-    def send_back(portion):
-        copies = []
+    back = {}
+
+    def send_back(portion, first, count):
         for o in range(1, n_seq):
             j = lax.rem(me + o, n_seq)
+            place = (portion, first // (tokens // 2), o - 1)
+            source = pl.ds(pl.multiple_of(j * tokens + first, 16), count)
             copy = remote(
-                gsend.at[portion, rows_of(j)], gback.at[portion, :, lanes_of(me)],
-                b_send.at[portion, o - 1], b_recv.at[portion, o - 1], "seq", j,
+                gsend.at[portion, source],
+                gback.at[portion, first : first + count, lanes_of(me)],
+                b_send.at[place], b_recv.at[place], along[o - 1],
             )
             copy.start()
-            copies.append(copy)
+            back.setdefault(place[:2], []).append(copy)
+
+    def keep_own(portion):
         gback[portion, :, lanes_of(me)] = gsend[portion, my_rows, :]
-        return copies
 
     for kind in (0, 1, 2):
         arrived(kind)
@@ -290,7 +297,8 @@
             else:
                 acc_v[:reach, :] += term
     gsend[2] = acc_v[...].astype(jnp.bfloat16)
-    back = {2: send_back(2)}
+    send_back(2, 0, tokens)
+    keep_own(2)
 
     arrived(3)
     for block in blocks:
@@ -311,84 +319,93 @@
             else:
                 acc_k[:reach, :] += term
         gsend[0, first:reach, :] = grad_query.astype(jnp.bfloat16)
-    back[0] = send_back(0)
     gsend[1] = acc_k[...].astype(jnp.bfloat16)
-    back[1] = send_back(1)
-
-    for portion in (2, 0, 1):
-        for copy in back[portion]:
+    part = tokens // 2
+    for first in (0, part):
+        for portion in (0, 1):
+            send_back(portion, first, part)
+    keep_own(0)
+    keep_own(1)
+
+    own_cut = pl.ds(pl.multiple_of(core * half, LANES), half)
+    exchanges, sums = {}, [0.0] * n_head
+
+    def make_partial(a):
+        rows = slice(a * part, (a + 1) * part)
+        for c in range(n_head):
+            cut = slice(c * half, (c + 1) * half)
+            partial = dot(gback[2, rows, :], w_ref[2, cut, :], NT)
+            for p in (0, 1):
+                partial = partial + dot(gback[p, rows, :], w_ref[p, cut, :], NT)
+            rounded = partial.astype(jnp.bfloat16)
+            part_out[a, c] = rounded
+            exchanges[a, c] = remote(
+                part_out.at[a, c], part_in.at[a, c], h_send.at[a, c], h_recv.at[a, c],
+                {"head": lax.rem(core + 1, n_head)},
+            )
+            exchanges[a, c].start()
+            sums[c] = sums[c] + jnp.sum(
+                rounded.astype(jnp.float32) * scaled_ref[rows, cut], 0, keepdims=True
+            )
+
+    def finish(a):
+        rows = slice(a * part, (a + 1) * part)
+        first_sum, second_sum = 0.0, 0.0
+        for c in range(n_head):
+            cut = slice(c * half, (c + 1) * half)
+            exchanges[a, c].wait_recv()
+            gradient = part_out[a, c].astype(jnp.float32) + part_in[a, c].astype(jnp.float32)
+            scaled_grad = gradient * gain_ref[:, cut]
+            first_sum = first_sum + jnp.sum(scaled_grad, -1, keepdims=True)
+            second_sum = second_sum + jnp.sum(scaled_grad * scaled_ref[rows, cut], -1, keepdims=True)
+        gradient = part_out[a, core].astype(jnp.float32) + part_in[a, core].astype(jnp.float32)
+        inner = gradient * gain_ref[:, own_cut] - first_sum / width
+        inner = inner - scaled_ref[rows, own_cut] * (second_sum / width)
+        grad_ref[rows, :] = (spread_ref[rows, :1] * inner).astype(jnp.bfloat16)
+
+    for place in ((2, 0), (0, 0), (1, 0)):
+        for copy in back[place]:
             copy.wait_recv()
-    exchanges = []
-    for c in range(2):
-        cut = slice(c * width // 2, (c + 1) * width // 2)
-        partial = dot(gback[0], w_ref[0, cut, :], NT)
-        for p in (1, 2):
-            partial = partial + dot(gback[p], w_ref[p, cut, :], NT)
-        part_out[c] = partial.astype(jnp.bfloat16)
-        copy = remote(
-            part_out.at[c], part_in.at[c], h_send.at[c], h_recv.at[c], "head", lax.rem(core + 1, n_head)
-        )
-        copy.start()
-        exchanges.append(copy)
-
-    gradients, first_sum, second_sum = [], 0.0, 0.0
-    for c in range(2):
-        cut = slice(c * width // 2, (c + 1) * width // 2)
-        exchanges[c].wait_recv()
-        gradient = part_out[c].astype(jnp.float32) + part_in[c].astype(jnp.float32)
-        scaled_grad = gradient * gain_ref[:, cut]
-        own_scaled = scaled_ref[:, cut]
-        first_sum = first_sum + jnp.sum(scaled_grad, -1, keepdims=True)
-        second_sum = second_sum + jnp.sum(scaled_grad * own_scaled, -1, keepdims=True)
-    own_cut = pl.ds(pl.multiple_of(core * half, LANES), half)
-    gradient = part_out[core].astype(jnp.float32) + part_in[core].astype(jnp.float32)
-    own_scaled = scaled_ref[:, own_cut]
-    local_sum = jnp.sum(gradient * own_scaled, 0, keepdims=True)
-    gain_src[...] = jnp.zeros_like(gain_src)
-    for c in range(half // LANES):
-        gain_src[c : c + 1, :] = local_sum[:, c * LANES : (c + 1) * LANES]
-    over_dp = []
-    for o in range(1, n_dp):
-        copy = remote(
-            gain_src, gain_dp.at[group], d_send.at[o - 1], d_recv.at[o - 1],
-            "dp", lax.rem(group + o, n_dp),
-        )
-        copy.start()
-        over_dp.append(copy)
-    gain_dp[group] = gain_src[...]
-    scaled_grad = gradient * gain_ref[:, own_cut]
-    first_mean = first_sum / width
-    second_mean = second_sum / width
-    again = hidden_ref[...].astype(jnp.float32)
-    again = again - jnp.mean(again, -1, keepdims=True)
-    spread = lax.rsqrt(jnp.mean(again * again, -1, keepdims=True) + epsilon)
-    grad_ref[...] = (spread * (scaled_grad - first_mean - own_scaled * second_mean)).astype(
-        jnp.bfloat16
-    )
-    for copy in over_dp:
+    make_partial(0)
+    finish(0)
+    for place in ((0, 1), (1, 1)):
+        for copy in back[place]:
+            copy.wait_recv()
+    make_partial(1)
+
+    half_rows = half // LANES
+    for c in range(n_head):
+        for i in range(half_rows):
+            at = c * half_rows + i
+            gain_src[at : at + 1, :] = sums[c][:, i * LANES : (i + 1) * LANES]
+    over_seq, over_rest = [], []
+    for o, peer in enumerate(along):
+        over_seq.append(remote(gain_src, gain_seq.at[me], s_send.at[o], s_recv.at[o], peer))
+        over_seq[-1].start()
+    gain_seq[me] = gain_src[...]
+    finish(1)
+    for copy in over_seq:
         copy.wait_recv()
-    total = gain_dp[0]
-    for j in range(1, n_dp):
-        total = total + gain_dp[j]
-    gain_mid[...] = total
-    over_seq = []
-    for o in range(1, n_seq):
-        copy = remote(
-            gain_mid, gain_seq.at[me], s_send.at[o - 1], s_recv.at[o - 1],
-            "seq", lax.rem(me + o, n_seq),
-        )
-        copy.start()
-        over_seq.append(copy)
-    gain_seq[me] = total
-    for copies in (label_copies, forward.values(), *back.values(), exchanges, over_dp):
-        for copy in copies:
-            copy.wait_send()
-    for copy in over_seq:
-        copy.wait()
     total = gain_seq[0]
     for j in range(1, n_seq):
         total = total + gain_seq[j]
-    gain_out_ref[...] = total * total_rows ** (-0.5)
+    gain_mid[...] = total
+    slot = group * n_head + core
+    for o, peer in enumerate(across):
+        over_rest.append(remote(gain_mid, gain_all.at[slot], d_send.at[o], d_recv.at[o], peer))
+        over_rest[-1].start()
+    gain_all[slot] = total
+    for copies in (label_copies, forward.values(), *back.values(), exchanges.values(), over_seq):
+        for copy in copies:
+            copy.wait_send()
+    for copy in over_rest:
+        copy.wait()
+    total = gain_all[0]
+    for j in range(1, n_dp * n_head):
+        total = total + gain_all[j]
+    gain_sum[...] = total * total_rows ** (-0.5)
+    for i in range(half_rows):
+        gain_out_ref[:, i * LANES : (i + 1) * LANES] = gain_sum[pl.ds(core * half_rows + i, 1), :]
 
 
 def on_device_heads(hidden, norm_gain, projection, upstream, cluster):
@@ -405,7 +422,7 @@
         cluster[0, :, 0].astype(jnp.float32),
         (lax.axis_index("seq") * tokens,),
     ).reshape(label_rows, LANES)
-    gain_rows = -(-half // (8 * LANES)) * 8
+    gain_rows = width // LANES
     vmem = pl.BlockSpec(memory_space=pltpu.VMEM)
     dma = pltpu.SemaphoreType.DMA
     bf16, f32 = jnp.bfloat16, jnp.float32
@@ -413,7 +430,7 @@
         functools.partial(fused, n_seq, n_head, n_dp, n_seq * n_dp * tokens),
         out_shape=(
             jax.ShapeDtypeStruct((tokens, half), bf16),
-            jax.ShapeDtypeStruct((gain_rows, LANES), f32),
+            jax.ShapeDtypeStruct((1, half), f32),
         ),
         in_specs=[vmem, vmem, pl.BlockSpec(memory_space=pl.ANY), vmem, vmem],
         out_specs=(vmem, vmem),
@@ -429,30 +446,31 @@
             pltpu.VMEM((length, LANES), f32),
             pltpu.VMEM((3, length, LANES), bf16),
             pltpu.VMEM((3, tokens, spans), bf16),
-            pltpu.VMEM((2, tokens, width // 2), bf16),
-            pltpu.VMEM((2, tokens, width // 2), bf16),
-            pltpu.VMEM((gain_rows, LANES), f32),
-            pltpu.VMEM((n_dp, gain_rows, LANES), f32),
+            pltpu.VMEM((2, n_head, tokens // 2, half), bf16),
+            pltpu.VMEM((2, n_head, tokens // 2, half), bf16),
+            pltpu.VMEM((tokens, LANES), f32),
             pltpu.VMEM((gain_rows, LANES), f32),
             pltpu.VMEM((n_seq, gain_rows, LANES), f32),
+            pltpu.VMEM((gain_rows, LANES), f32),
+            pltpu.VMEM((n_dp * n_head, gain_rows, LANES), f32),
+            pltpu.VMEM((gain_rows, LANES), f32),
             dma((3,)),
             dma((4, n_seq - 1)),
             dma((4, n_seq - 1)),
             dma((n_seq - 1,)),
             dma((n_seq - 1,)),
-            dma((3, n_seq - 1)),
-            dma((3, n_seq - 1)),
-            dma((2,)),
-            dma((2,)),
-            dma((n_dp - 1,)),
-            dma((n_dp - 1,)),
+            dma((3, 2, n_seq - 1)),
+            dma((3, 2, n_seq - 1)),
+            dma((2, n_head)),
+            dma((2, n_head)),
             dma((n_seq - 1,)),
             dma((n_seq - 1,)),
+            dma((n_dp * n_head - 1,)),
+            dma((n_dp * n_head - 1,)),
         ],
         compiler_params=pltpu.CompilerParams(collective_id=0, has_side_effects=True),
     )(hidden[0], norm_gain[None, :], projection, upstream[0], labels)
-    gain_gradient = gain[: half // LANES].reshape(half)
-    return (gradient.reshape(1, tokens, half), gain_gradient)
+    return (gradient.reshape(1, tokens, half), gain.reshape(half))
 
 
 def splits_by_heads(mesh, hidden, projection):

time: 55.4 us -> 54.5 us (0.984)
  Pallas kernels: 50.2 us -> 49.3 us
    reshape x1 -> x0, local copies, waits for them, and re-layouts: 1.25 us -> none  [on_device_heads(): gain_gradient = gain[:half // LANES].reshape(half)]
    unnamed x3 -> x4, local copies, waits for them, and re-layouts: 2.21 us -> 3.44 us
    pallas_call x1, Pallas kernels: 50.2 us -> 49.3 us  [on_device_heads(): pl.pallas_call(functools.partial(fused, n_seq, n_head, n_dp, n_seq * n_dp...]
where the time goes in v2:
time: 54.5 us; the launch traced here: 54.2 us
  Pallas kernels  49.3 us (90%)
  local copies, waits for them, and re-layouts  3.62 us (7%)
  other arithmetic  0.68 us (1%)
  between operations  0.65 us (1%)
    pallas_call x1, Pallas kernels, on_device_heads(): pl.pallas_call(functools.partial(fused, n_seq, n_head, n_dp, n_seq * n_dp...  49.3 us
    unnamed x4, local copies, waits for them, and re-layouts  3.44 us

profile of v2, /device:TPU:0, one launch (start us, length us, event | category | flops | bytes accessed | tf_op | source)
XLA Modules:
  0.0 54.2 jit_solution(12990994755411764875)
XLA Ops:
  0.6 0.7 %convert_element_type.6 = f32[1,192,1]{1,2,0:T(1,128)S(1)} convert(s32[1,192,1]{1,2,0:T(1,128)} %param.9) | non-fusion elementwise | flops 192 | bytes 1536 | tf_op jit(solution)/shard_map/convert_element_type | solution.py:422
  1.3 0.2 dynamic_update_slice.3
  1.5 0.0 copy-start
  1.5 0.6 %copy-done = f32[1024]{0:T(1024)} copy-done((f32[1024]{0:T(1024)}, f32[1024]{0:T(1024)S(1)}, u32[]{:S(2)}) %copy-start) | copy-done | bytes 4120
  2.1 49.3 %shard_map.68 = (bf16[192,512]{1,0:T(8,128)(2,1)}, f32[1,512]{1,0:T(1,128)}) custom-call(bf16[192,1024]{1,0:T(8,128)(2,1)} %bitcast.7, f32[1,1024]{1,0:T(1,128)} %bitcast.11, bf16[3,1024,512]{2,1,0:T(8,128)(2,1)} %proj_hbm.1, bf16[192,512]{1,0:T(8,128)(2,1)} %bitcast.8, f32[8,128]{1,0:T(8,128)} %bitcast.10), custom_call_target="tpu_custom_call" | custom-call | tf_op jit(solution)/shard_map/pallas_call | solution.py:429
  51.4 1.6 %copy.10 = bf16[1,192,512]{2,1,0:T(8,128)(2,1)} copy(bf16[1,192,512]{2,1,0:T(8,128)(2,1)} %bitcast.9) | data formatting | bytes 393216
  53.0 1.2 %copy.11 = f32[512]{0:T(512)} copy(f32[512]{0:T(512)} %bitcast.13) | data formatting | bytes 4096
  (1 shorter events, 0.0 us)
Async XLA Ops:
  1.5 0.6 %copy-start = (f32[1024]{0:T(1024)}, f32[1024]{0:T(1024)S(1)}, u32[]{:S(2)}) copy-start(f32[1024]{0:T(1024)S(1)} %dynamic_update_slice.3) | copy-start | bytes 12292
